TPU v7x, 512 devices: a whole 4x4x16 slice. The times are simulated.
512 devices in a mesh: row: 32 (over z_hi, y, core), col: 16 (over z_lo, x).
Axes of the slice: x: 4, y: 4, z: 16 (z_hi: 4, z_lo: 4; z = z_hi * 4 + z_lo), core: 2. Of those that a mesh axis runs over, the one named last changes fastest.
Arguments:
- hidden: bfloat16 [256, 2048], P('row', 'col'), may hold values from -60 to 60
- queries: bfloat16 [256, 4096], P('row'), may hold values from -6 to 6
- new_kv: bfloat16 [256, 2, 2048], P('row'), may hold values from -12 to 12
- prompt_kv: bfloat16 [32, 2, 1024, 2048], P('row', None, 'col'), may hold values from -180 to 180
- suffix_kv: bfloat16 [256, 2, 128, 2048], P('row', None, 'col'), may hold values from -12 to 12
- lengths: int32 [256], P('row'), may hold values from 1 to 128, as said below
- w_out: bfloat16 [4096, 2048], P(None, 'col'), may hold values from -0.375 to 0.375
- moe_gain: bfloat16 [2048], P('col'), may hold values from 0.099609375 to 1.8984375
- w_router: bfloat16 [2048, 8], P('col'), may hold values from -0.5 to 0.5
- expert_weights: bfloat16 [8, 5632, 3, 2048], P(None, 'row', None, 'col'), may hold values from -0.25 to 0.25
- old_lines: int32 [8, 5632], replicated, may hold values from 0 to 5631, as said below
- new_lines: int32 [8, 5632], replicated, may hold values from 0 to 5631, as said below
- routes: int32 [256, 2], replicated, may hold values from 0 to 7, all different within a row
Outputs:
- layer_out: float32 [256, 2048], P('row', 'col')
- moved_weights: bfloat16 [8, 5632, 3, 2048], P(None, 'row', None, 'col')
Inputs may be any that keep to these rules, and one draw needn't show every extreme that they name: `lengths`: some sequence has all 128 slots filled. `old_lines`: each row is a permutation of the hidden units of one expert; stored lines [j * 176, (j + 1) * 176) lie on row index j. `new_lines`: each row is a permutation of the hidden units of one expert. Counting all experts together, exactly 44 of the lines that one row index holds under old_lines are held by each row index under new_lines. `routes`: the two experts of a token differ.
All inputs are finite; a program needn't handle non-finite values.
Results may differ from a plain program's by a relative error of at most 0.04.
Values may be sent and summed in bfloat16 or wider, within the bound.
A program may use at most 64 MiB of HBM per device.

v0:
```python
import jax
import jax.numpy as jnp
from jax import lax
from jax.sharding import PartitionSpec as P

D = 2048
KVH = 16
HD = 128
REP = 2
norm_eps = 1e-06
neg_big = -1e30


def joined(part, axis, combine):
    gathered = jax.tree.map(lambda a: lax.all_gather(a, axis), part)

    def take(source):
        return jax.tree.map(lambda a: lax.dynamic_index_in_dim(a, source, 0, False), gathered)

    return lax.fori_loop(
        1, lax.axis_size(axis), lambda source, state: combine(state, take(source)), take(0)
    )


def merge_partial(earlier, following):
    highest_a, totals_a, mixture_a = earlier
    highest_b, totals_b, mixture_b = following
    highest = jnp.maximum(highest_a, highest_b)
    factor_a = jnp.exp(highest_a - highest)
    factor_b = jnp.exp(highest_b - highest)
    return (
        highest,
        totals_a * factor_a + totals_b * factor_b,
        mixture_a * factor_a[..., None] + mixture_b * factor_b[..., None],
    )


def attend(queries, new_kv, prompt_kv, suffix_kv, lengths):
    seq_count = queries.shape[0]
    prompt_rows = prompt_kv.shape[2]
    suffix_rows = suffix_kv.shape[2]
    col_index = lax.axis_index("col")
    query_heads = queries.reshape(seq_count, KVH, REP, HD)
    prompt_keys = prompt_kv[0, 0].reshape(prompt_rows, KVH, HD)
    prompt_values = prompt_kv[0, 1].reshape(prompt_rows, KVH, HD)
    suffix_keys = suffix_kv[:, 0].reshape(seq_count, suffix_rows, KVH, HD)
    suffix_values = suffix_kv[:, 1].reshape(seq_count, suffix_rows, KVH, HD)
    own_keys = new_kv[:, 0].reshape(seq_count, KVH, HD)
    own_values = new_kv[:, 1].reshape(seq_count, KVH, HD)
    score_scale = HD ** (-0.5)
    prompt_scores = (
        jnp.einsum("skgd,pkd->skgp", query_heads, prompt_keys, preferred_element_type=jnp.float32)
        * score_scale
    )
    suffix_scores = (
        jnp.einsum("skgd,spkd->skgp", query_heads, suffix_keys, preferred_element_type=jnp.float32)
        * score_scale
    )
    own_scores = (
        jnp.einsum("skgd,skd->skg", query_heads, own_keys, preferred_element_type=jnp.float32)
        * score_scale
    )
    positions = col_index * suffix_rows + jnp.arange(suffix_rows, dtype=jnp.int32)
    live_slots = (positions[None, :] < lengths[:, None])[:, None, None, :]
    holder = col_index == 0
    suffix_scores = jnp.where(live_slots, suffix_scores, neg_big)
    own_scores = jnp.where(holder, own_scores, neg_big)
    highest = jnp.maximum(
        jnp.maximum(jnp.max(prompt_scores, axis=-1), jnp.max(suffix_scores, axis=-1)), own_scores
    )
    prompt_weights = jnp.exp(prompt_scores - highest[..., None])
    suffix_weights = jnp.where(live_slots, jnp.exp(suffix_scores - highest[..., None]), 0.0)
    own_weights = jnp.where(holder, jnp.exp(own_scores - highest), 0.0)
    totals = jnp.sum(prompt_weights, axis=-1) + jnp.sum(suffix_weights, axis=-1) + own_weights
    mixture = jnp.einsum(
        "skgp,pkd->skgd",
        prompt_weights.astype(jnp.bfloat16),
        prompt_values,
        preferred_element_type=jnp.float32,
    )
    mixture = mixture + jnp.einsum(
        "skgp,spkd->skgd",
        suffix_weights.astype(jnp.bfloat16),
        suffix_values,
        preferred_element_type=jnp.float32,
    )
    own_rounded = lax.optimization_barrier(own_weights.astype(jnp.bfloat16)).astype(jnp.float32)
    mixture = mixture + own_rounded[..., None] * own_values.astype(jnp.float32)[:, :, None, :]
    highest, totals, mixture = joined((highest, totals, mixture), "col", merge_partial)
    return (mixture / totals[..., None]).astype(jnp.bfloat16).reshape(seq_count, -1)


def inverse_rows(table):
    expert_count, full_width = table.shape
    row_ids = jnp.broadcast_to(jnp.arange(expert_count, dtype=jnp.int32)[:, None], table.shape)
    slot_ids = jnp.broadcast_to(jnp.arange(full_width, dtype=jnp.int32)[None, :], table.shape)
    return jnp.zeros_like(table).at[row_ids, table].set(slot_ids)


def migrate(expert_weights, old_lines, new_lines):
    row_count = lax.axis_size("row")
    row_index = lax.axis_index("row")
    expert_count, line_count, three_parts, width_col = expert_weights.shape
    full_width = old_lines.shape[1]
    unit_count = expert_count * line_count
    per_peer = unit_count // row_count
    inverse_old = inverse_rows(old_lines)
    inverse_new = inverse_rows(new_lines)
    held_ids = lax.dynamic_slice_in_dim(old_lines, row_index * line_count, line_count, 1)
    target_slots = jnp.take_along_axis(inverse_new, held_ids, axis=1)
    expert_ids = jnp.arange(expert_count, dtype=jnp.int32)[:, None]
    sort_keys = (
        target_slots // line_count * (expert_count * full_width)
        + expert_ids * full_width
        + target_slots
    )
    sort_order = jnp.argsort(sort_keys.reshape(-1))
    flat_units = expert_weights.reshape(unit_count, three_parts, width_col)
    outgoing = flat_units[sort_order].reshape(row_count, per_peer, three_parts, width_col)
    arrived = lax.all_to_all(outgoing, "row", split_axis=0, concat_axis=0, tiled=True).reshape(
        unit_count, three_parts, width_col
    )
    wanted_ids = lax.dynamic_slice_in_dim(new_lines, row_index * line_count, line_count, 1)
    anchor_rows = (jnp.take_along_axis(inverse_old, wanted_ids, axis=1) // line_count).reshape(-1)
    anchor_hits = (anchor_rows[:, None] == jnp.arange(row_count, dtype=jnp.int32)[None, :]).astype(
        jnp.int32
    )
    rank_within = jnp.sum(jnp.cumsum(anchor_hits, axis=0) * anchor_hits, axis=1) - 1
    arrived_slot = anchor_rows * per_peer + rank_within
    return arrived[arrived_slot].reshape(expert_count, line_count, three_parts, width_col)


def activate(summed, router_sum, square_sum, chosen):
    inverse_rms = lax.rsqrt(square_sum / D + norm_eps)
    logits = router_sum * inverse_rms[:, None]
    expert_hits = chosen[:, :, None] == jnp.arange(logits.shape[1], dtype=jnp.int32)[None, None, :]
    selected = jnp.sum(jnp.where(expert_hits, logits[:, None, :], 0.0), axis=-1)
    gates = jax.nn.softmax(selected, axis=-1)
    gate_part = summed[:, :, 0] * inverse_rms[:, None, None]
    up_part = summed[:, :, 1] * inverse_rms[:, None, None]
    activated = (jax.nn.silu(gate_part) * up_part).astype(jnp.bfloat16)
    return (gates, activated)


def local(
    hidden,
    queries,
    new_kv,
    prompt_kv,
    suffix_kv,
    lengths,
    w_out,
    moe_gain,
    w_router,
    expert_weights,
    old_lines,
    new_lines,
    routes,
):
    moved_weights = migrate(expert_weights, old_lines, new_lines)
    attended = attend(queries, new_kv, prompt_kv, suffix_kv, lengths)
    projected = jnp.dot(attended, w_out, preferred_element_type=jnp.float32)
    h_mid = (hidden.astype(jnp.float32) + projected).astype(jnp.bfloat16)
    h_float = h_mid.astype(jnp.float32)
    scaled = (h_float * moe_gain.astype(jnp.float32)[None, :]).astype(jnp.bfloat16)
    squares = jnp.sum(h_float * h_float, axis=1)
    every_token, every_square = (
        lax.all_gather(scaled, "row", axis=0, tiled=True),
        lax.all_gather(squares.astype(jnp.bfloat16), "row", axis=0, tiled=True).astype(
            squares.dtype
        ),
    )
    token_total = every_token.shape[0]
    router_part = jnp.dot(every_token, w_router, preferred_element_type=jnp.float32)
    gate_up = jnp.einsum(
        "td,efjd->etjf",
        every_token,
        expert_weights[:, :, :2, :],
        preferred_element_type=jnp.float32,
    )
    picked = gate_up[routes, jnp.arange(token_total, dtype=jnp.int32)[:, None]]
    summed, router_sum, square_sum = lax.psum((picked, router_part, every_square), "col")
    gates, activated = activate(summed, router_sum, square_sum, routes)
    down_lines = expert_weights[:, :, 2, :]
    top_count = routes.shape[1]
    every_expert = jnp.einsum(
        "tkf,efd->etkd", activated, down_lines, preferred_element_type=jnp.float32
    )
    chosen_out = every_expert[
        routes,
        jnp.arange(hidden.shape[0] * lax.axis_size("row"), dtype=jnp.int32)[:, None],
        jnp.arange(top_count, dtype=jnp.int32)[None, :],
    ]
    mixed = lax.psum_scatter(
        jnp.sum(chosen_out * gates[:, :, None], axis=1), "row", scatter_dimension=0, tiled=True
    )
    layer_out = h_float + mixed
    return (layer_out, moved_weights)


def solution(mesh):
    return jax.shard_map(
        local,
        mesh=mesh,
        in_specs=(
            P("row", "col"),
            P("row", None),
            P("row", None, None),
            P("row", None, "col", None),
            P("row", None, "col", None),
            P("row"),
            P(None, "col"),
            P("col"),
            P("col", None),
            P(None, "row", None, "col"),
            P(),
            P(),
            P(),
        ),
        out_specs=(P("row", "col"), P(None, "row", None, "col")),
        check_vma=False,
    )
```

profile of v0, /device:TPU:1, one launch (start us, length us, event | category | flops | bytes accessed | tf_op | source)
XLA Modules:
  0.0 1099.8 jit_solution(18043587728457277030)
XLA Ops:
  12.7 6.7 copy.177
  21.3 165.0 %scatter_custom_fusion = s32[45056]{0:T(1024)S(1)} fusion(s32[45056]{0:T(1024)} %reshape.244, s32[45056]{0:T(1024)} %reshape.246, s32[]{:T(128)} %constant.115.clone.1), kind=kCustom, calls=%fused_computation.72 | custom fusion | bytes 180736
  187.2 8.6 gather_fusion.4
  196.1 5.0 sort.17
  201.1 5.2 gather_fusion.2
  206.3 2.6 copy.179
  208.9 19.4 %all-to-all-start = ((bf16[32,44,3,128]{3,1,2,0:T(8,128)(2,1)}), bf16[32,44,3,128]{3,1,2,0:T(8,128)(2,1)}, u32[]{:S(2)}, u32[]{:S(2)}) async-start(bf16[32,44,3,128]{3,1,2,0:T(8,128)(2,1)} %copy.179), calls=%async_computation | async-start | bytes 2359296 | tf_op jit(solution)/shard_map/all_to_all | solution.py:120
  228.4 165.3 %scatter_custom_fusion.1 = s32[45056]{0:T(1024)S(1)} fusion(s32[45056]{0:T(1024)S(1)} %reshape.250, s32[45056]{0:T(1024)} %reshape.246, s32[]{:T(128)} %constant.115.clone.1), kind=kCustom, calls=%fused_computation.70 | custom fusion | bytes 180736
  393.9 8.6 gather_fusion.5
  403.6 34.4 %all-gather = f32[128,16,2]{1,2,0:T(2,128)S(1)} all-gather(f32[8,16,2]{1,2,0:T(2,128)S(1)} %copy.156), channel_id=2, replica_groups=mesh['row'=32,'col'=16] {'col'}, dimensions={0}, use_global_device_ids=true | all-gather | bytes 17408 | tf_op jit(solution)/shard_map/all_gather | solution.py:15
  438.9 30.4 %all-gather.1 = f32[128,16,2]{1,2,0:T(2,128)S(1)} all-gather(f32[8,16,2]{1,2,0:T(2,128)S(1)} %copy.161), channel_id=3, replica_groups=mesh['row'=32,'col'=16] {'col'}, dimensions={0}, use_global_device_ids=true | all-gather | bytes 17408 | tf_op jit(solution)/shard_map/all_gather | solution.py:15
  470.6 9.1 reduce-window.6
  482.6 30.4 %while.19 = (s32[]{:T(128)}, f32[8,16,2]{1,2,0:T(2,128)S(1)}, f32[8,16,2]{1,2,0:T(2,128)S(1)}, f32[8,16,2,128]{3,2,1,0:T(2,128)S(1)}, f32[16,8,16,2]{2,3,1,0:T(2...) while((s32[]{:T(128)}, f32[8,16,2]{1,2,0:T(2,128)S(1)}, ...), condition=%wide.region_5.6_spmd, body=%wide.region_4.5_spmd.sunk | while | flops 99845 | bytes 669847 | solution.py:20
  513.8 68.4 %all_gather.30 = bf16[256,128]{1,0:T(8,128)(2,1)S(1)} all-gather(bf16[8,128]{1,0:T(8,128)(2,1)S(1)} %get-tuple-element.267), channel_id=1, replica_groups=mesh['row'=32,'col'=16] {'row'}, dimensions={0}, use_global_device_ids=true | all-gather | bytes 67584 | tf_op jit(solution)/shard_map/all_gather | solution.py:168
  582.2 2.1 convolution_bitcast_fusion
  584.3 6.9 copy.170
  591.2 5.1 gather_fusion
  598.0 83.8 %all-reduce = bf16[256]{0:T(256)(128)(2,1)S(1)} all-reduce(bf16[256]{0:T(256)(128)(2,1)S(1)} %dynamic-update-slice), channel_id=1, replica_groups=mesh['row'=32,'col'=16] {'row'}, use_global_device_ids=true, to_apply=%add | all-reduce | flops 256 | bytes 1024
  681.9 33.7 %all-reduce.2 = (f32[256]{0:T(256)S(1)}, f32[256,8]{0,1:T(8,128)S(1)}) all-reduce(bf16[256]{0:T(256)(128)(2,1)S(1)} %all-reduce, f32[256,8]{0,1:T(8,128)S(1)} %fusion.62), channel_id=1, replica_groups=mesh['row'=32,'col'=16] {'col'}, use_global_device_ids=true, to_apply=%region_8.9 | all-reduce | flops 2304 | bytes 17920 | tf_op jit(solution)/shard_map/psum | solution.py:182
  715.9 36.3 %all-reduce.6.cloned.1.call-done = f32[256,2,2,176]{0,3,2,1:T(8,128)} async-done(((f32[256,2,2,176]{0,3,2,1:T(8,128)}), f32[256,2,2,176]{0,3,2,1:T(8,128)}) %all-reduce.6.cloned.1.call-update) | async-done | bytes 720912 | tf_op jit(solution)/shard_map/psum | solution.py:182
  755.4 2.9 gather_fusion.1
  762.6 5.2 gather_fusion.3
  767.7 2.5 copy.185
  770.2 321.7 %all-reduce.8.cloned.1.call-done = f32[256,128]{1,0:T(8,128)} async-done(((f32[256,128]{1,0:T(8,128)}), f32[256,128]{1,0:T(8,128)}) %all-reduce.8.cloned.1.call-update) | async-done | bytes 131088
  (218 shorter events, 54.7 us)
Async XLA Ops:
  7.2 506.3 %copy-start = (bf16[4096,128]{1,0:T(8,128)(2,1)S(1)}, bf16[4096,128]{1,0:T(8,128)(2,1)}, u32[]{:S(2)}) copy-start(bf16[4096,128]{1,0:T(8,128)(2,1)} %param.23) | copy-start | bytes 3145732
  7.2 2.6 copy-start.8
  7.2 3.0 copy-start.16
  7.2 3.1 copy-start.18
  7.2 474.4 %all-gather.5.cloned.1.call-start = ((), (), s32[]{:S(2)}) async-start(), calls=%async_computation.2 | async-start | bytes 2228224 | tf_op jit(solution)/shard_map/all_gather | solution.py:15
  9.7 1.3 copy-start.7
  10.3 1.3 copy-start.10
  10.9 1.7 copy-start.5
  11.2 1.3 copy-start.1
  12.6 6.8 copy-start.3
  12.6 6.8 copy-start.4
  12.7 6.9 copy-start.17
  12.7 7.0 copy-start.14
  208.9 551.8 %all-to-all-start = ((bf16[32,44,3,128]{3,1,2,0:T(8,128)(2,1)}), bf16[32,44,3,128]{3,1,2,0:T(8,128)(2,1)}, u32[]{:S(2)}, u32[]{:S(2)}) async-start(bf16[32,44,3,128]{3,1,2,0:T(8,128)(2,1)} %copy.179), calls=%async_computation | async-start | bytes 2359296 | tf_op jit(solution)/shard_map/all_to_all | solution.py:120
  228.3 523.8 %all-reduce.6.cloned.1.call-start = ((), (), s32[]{:S(2)}) async-start(), calls=%async_computation.1 | async-start | bytes 1441792 | tf_op jit(solution)/shard_map/psum | solution.py:182
  393.9 9.7 copy-start.19
  393.9 44.1 %copy-start.6 = (f32[8,16,2]{0,2,1:T(2,128)S(1)}, f32[8,16,2]{0,2,1:T(2,128)}, u32[]{:S(2)}) copy-start(f32[8,16,2]{0,2,1:T(2,128)} %copy-done.5) | copy-start | bytes 3076
  393.9 44.4 %copy-start.11 = (pred[8,8]{1,0:T(8,128)(4,1)S(1)}, pred[8,8]{1,0:T(8,128)(4,1)}, u32[]{:S(2)}) copy-start(pred[8,8]{1,0:T(8,128)(4,1)} %copy-done.10) | copy-start | bytes 196
  393.9 75.4 %copy-start.9 = (s32[256,2]{0,1:T(2,128)S(1)}, s32[256,2]{0,1:T(2,128)}, u32[]{:S(2)}) copy-start(s32[256,2]{0,1:T(2,128)} %param.29) | copy-start | bytes 6148
  438.0 42.1 %copy-start.15 = (u32[512]{0:T(512)S(1)}, u32[512]{0:T(512)}, u32[]{:S(2)}) copy-start(u32[512]{0:T(512)} %constant.216) | copy-start | bytes 6148
  482.6 30.8 %copy-start.12 = (bf16[8,128]{1,0:T(8,128)(2,1)S(1)}, bf16[8,128]{1,0:T(8,128)(2,1)}, u32[]{:S(2)}) copy-start(bf16[8,128]{1,0:T(8,128)(2,1)} %param.17) | copy-start | bytes 6148
  513.0 69.2 %copy-start.2 = (bf16[8,176,3,128]{3,1,2,0:T(8,128)(2,1)S(1)}, bf16[8,176,3,128]{3,1,2,0:T(8,128)(2,1)}, u32[]{:S(2)}) copy-start(bf16[8,176,3,128]{3,1,2,0:T(8,128)(2,1)} %param.26) | copy-start | bytes 3244036
  596.3 85.5 %copy-start.13 = (bf16[128,8]{0,1:T(8,128)(2,1)S(1)}, bf16[128,8]{0,1:T(8,128)(2,1)}, u32[]{:S(2)}) copy-start(bf16[128,8]{0,1:T(8,128)(2,1)} %param.25) | copy-start | bytes 6148
  597.7 494.3 %all-reduce.8.cloned.1.call-start = ((), (), s32[]{:S(2)}) async-start(), calls=%async_computation.3 | async-start | bytes 262144
Sparse Core Ops, SparseCore 0:
  12.7 75.4 all-gather.4
  597.8 154.3 all-reduce.5
  759.4 332.4 all-reduce.7
where the time goes:
time: 1100 us
  local copies, waits for them, and re-layouts  415 us (38%)
  waiting for transfers between devices  358 us (33%)
  blocking collectives  251 us (23%)
  other arithmetic  33.2 us (3%)
  starting transfers between devices  19.6 us (2%)
  between operations  15.8 us (1%)
    unnamed x52, local copies, waits for them, and re-layouts  336 us
    unnamed x4, waiting for transfers between devices  322 us
    unnamed x1, blocking collectives  83.8 us
    all_gather x1, blocking collectives, local(): lax.all_gather(scaled, 'row', axis=0, tiled=True)  68.4 us
    all_gather x2, blocking collectives, joined(): gathered = jax.tree.map(lambda a: lax.all_gather(a, axis), part)  64.9 us
    psum x1, waiting for transfers between devices, local(): lax.psum((picked, router_part, every_square), 'col')  36.3 us
    psum x1, blocking collectives, local(): lax.psum((picked, router_part, every_square), 'col')  33.7 us
  transfers between devices with their start and end apart: 4, of which 2 were waited for; matrix products, arithmetic and copies ran while one was open for 41% of the time, Pallas kernels for 0%

commit v1 on v0

--- a/solution.py
+++ b/solution.py
@@ -157,6 +157,13 @@
     new_lines,
     routes,
 ):
+
+    def attach_gates(u, bus_axis):
+        built = lax.axis_size(bus_axis)
+        v_next = jnp.stack(built * [u])
+        carry = lax.all_to_all(v_next, axis_name=bus_axis, concat_axis=0, split_axis=0)
+        return jnp.concatenate(carry, axis=0)
+
     moved_weights = migrate(expert_weights, old_lines, new_lines)
     attended = attend(queries, new_kv, prompt_kv, suffix_kv, lengths)
     projected = jnp.dot(attended, w_out, preferred_element_type=jnp.float32)
@@ -165,7 +172,7 @@
     scaled = (h_float * moe_gain.astype(jnp.float32)[None, :]).astype(jnp.bfloat16)
     squares = jnp.sum(h_float * h_float, axis=1)
     every_token, every_square = (
-        lax.all_gather(scaled, "row", axis=0, tiled=True),
+        attach_gates(scaled, "row"),
         lax.all_gather(squares.astype(jnp.bfloat16), "row", axis=0, tiled=True).astype(
             squares.dtype
         ),

time: 1100 us -> 1150 us (1.045)
  waiting for transfers between devices: 358 us -> 456 us
  blocking collectives: 251 us -> 188 us
  starting transfers between devices: 19.6 us -> 36.2 us
    psum x1, waiting for transfers between devices: 36.3 us -> 128 us  [local(): lax.psum((picked, router_part, every_square), 'col')]
    all_gather x1 -> x0, blocking collectives: 68.4 us -> none  [local(): lax.all_gather(scaled, 'row', axis=0, tiled=True)]
    all_to_all x0 -> x1, starting transfers between devices: none -> 28.3 us  [attach_gates(): lax.all_to_all(v_next, axis_name=bus_axis, concat_axis=0, split_axis=0)]
    all_to_all x1, starting transfers between devices: 19.4 us -> 7.78 us  [migrate(): lax.all_to_all(outgoing, 'row', split_axis=0, concat_axis=0, tiled=True)]
    unnamed x52 -> x46, local copies, waits for them, and re-layouts: 336 us -> 336 us
  transfers between devices with their start and end apart: 4 -> 5, of which waited for: 2 -> 3; matrix products, arithmetic and copies ran while one was open for 41% -> 36% of each run, Pallas kernels for 0% -> 0%
where the time goes in v1:
time: 1150 us
  waiting for transfers between devices  456 us (40%)
  local copies, waits for them, and re-layouts  415 us (36%)
  blocking collectives  188 us (16%)
  starting transfers between devices  36.2 us (3%)
  other arithmetic  33.6 us (3%)
  between operations  15.8 us (1%)
    unnamed x46, local copies, waits for them, and re-layouts  336 us
    unnamed x4, waiting for transfers between devices  322 us
    psum x1, waiting for transfers between devices, local(): lax.psum((picked, router_part, every_square), 'col')  128 us
    unnamed x1, blocking collectives  84.1 us
    all_gather x2, blocking collectives, joined(): gathered = jax.tree.map(lambda a: lax.all_gather(a, axis), part)  70.1 us
    psum x1, blocking collectives, local(): lax.psum((picked, router_part, every_square), 'col')  34.1 us
    all_to_all x1, starting transfers between devices, attach_gates(): lax.all_to_all(v_next, axis_name=bus_axis, concat_axis=0, split_axis=0)  28.3 us
  transfers between devices with their start and end apart: 5, of which 3 were waited for; matrix products, arithmetic and copies ran while one was open for 36% of the time, Pallas kernels for 0%

profile of v1, /device:TPU:1, one launch (start us, length us, event | category | flops | bytes accessed | tf_op | source)
XLA Modules:
  0.0 1153.4 jit_solution(12342489374919547473)
XLA Ops:
  13.1 38.4 %all-gather = f32[128,16,2]{1,2,0:T(2,128)S(1)} all-gather(f32[8,16,2]{1,2,0:T(2,128)S(1)} %copy.156), channel_id=2, replica_groups=mesh['row'=32,'col'=16] {'col'}, dimensions={0}, use_global_device_ids=true | all-gather | bytes 17408 | tf_op jit(solution)/shard_map/all_gather | solution.py:15
  52.3 31.7 %all-gather.1 = f32[128,16,2]{1,2,0:T(2,128)S(1)} all-gather(f32[8,16,2]{1,2,0:T(2,128)S(1)} %copy.161), channel_id=3, replica_groups=mesh['row'=32,'col'=16] {'col'}, dimensions={0}, use_global_device_ids=true | all-gather | bytes 17408 | tf_op jit(solution)/shard_map/all_gather | solution.py:15
  84.2 6.7 copy.177
  92.8 165.0 %scatter_custom_fusion = s32[45056]{0:T(1024)S(1)} fusion(s32[45056]{0:T(1024)} %reshape.250, s32[45056]{0:T(1024)} %reshape.252, s32[]{:T(128)} %constant.115.clone.1), kind=kCustom, calls=%fused_computation.72 | custom fusion | bytes 180736
  258.7 8.6 gather_fusion.4
  267.6 5.0 sort.17
  273.6 30.3 %while.19 = (s32[]{:T(128)}, f32[8,16,2]{1,2,0:T(2,128)S(1)}, f32[8,16,2]{1,2,0:T(2,128)S(1)}, f32[8,16,2,128]{3,2,1,0:T(2,128)S(1)}, f32[16,8,16,2]{2,3,1,0:T(2...) while((s32[]{:T(128)}, f32[8,16,2]{1,2,0:T(2,128)S(1)}, ...), condition=%wide.region_5.6_spmd, body=%wide.region_4.5_spmd.sunk | while | flops 99845 | bytes 669847 | solution.py:20
  305.4 28.3 %all-to-all-start = ((bf16[32,8,128]{2,1,0:T(8,128)(2,1)}), bf16[32,8,128]{2,1,0:T(8,128)(2,1)S(1)}, u32[]{:S(2)}, u32[]{:S(2)}) async-start(bf16[32,8,128]{2,1,0:T(8,128)(2,1)} %stack.2), calls=%async_computation | async-start | bytes 131072 | tf_op jit(solution)/shard_map/all_to_all | solution.py:164
  333.6 5.2 gather_fusion.2
  338.8 2.6 copy.179
  341.4 6.9 all-to-all-done
  348.2 7.8 all-to-all-start.1
  356.1 165.3 %scatter_custom_fusion.1 = s32[45056]{0:T(1024)S(1)} fusion(s32[45056]{0:T(1024)S(1)} %reshape.256, s32[45056]{0:T(1024)} %reshape.252, s32[]{:T(128)} %constant.115.clone.1), kind=kCustom, calls=%fused_computation.70 | custom fusion | bytes 180736
  521.6 8.6 gather_fusion.5
  532.5 9.1 reduce-window.6
  543.8 84.1 %all-reduce = bf16[256]{0:T(256)(128)(2,1)S(1)} all-reduce(bf16[256]{0:T(256)(128)(2,1)S(1)} %dynamic-update-slice), channel_id=1, replica_groups=mesh['row'=32,'col'=16] {'row'}, use_global_device_ids=true, to_apply=%add | all-reduce | flops 256 | bytes 1024
  630.1 6.9 copy.170
  636.9 5.1 gather_fusion
  643.6 34.1 %all-reduce.2 = (f32[256]{0:T(256)S(1)}, f32[256,8]{0,1:T(8,128)S(1)}) all-reduce(bf16[256]{0:T(256)(128)(2,1)S(1)} %all-reduce, f32[256,8]{0,1:T(8,128)S(1)} %fusion.36), channel_id=1, replica_groups=mesh['row'=32,'col'=16] {'col'}, use_global_device_ids=true, to_apply=%region_8.9 | all-reduce | flops 2304 | bytes 17920 | tf_op jit(solution)/shard_map/psum | solution.py:189
  677.9 127.8 %all-reduce.6.cloned.1.call-done = f32[256,2,2,176]{0,3,2,1:T(8,128)} async-done(((f32[256,2,2,176]{0,3,2,1:T(8,128)}), f32[256,2,2,176]{0,3,2,1:T(8,128)}) %all-reduce.6.cloned.1.call-update) | async-done | bytes 720912 | tf_op jit(solution)/shard_map/psum | solution.py:189
  808.9 2.9 gather_fusion.1
  816.1 5.2 gather_fusion.3
  821.3 2.5 copy.185
  823.8 321.8 %all-reduce.8.cloned.1.call-done = f32[256,128]{1,0:T(8,128)} async-done(((f32[256,128]{1,0:T(8,128)}), f32[256,128]{1,0:T(8,128)}) %all-reduce.8.cloned.1.call-update) | async-done | bytes 131088
  (214 shorter events, 57.9 us)
Async XLA Ops:
  7.2 297.2 %copy-start = (bf16[4096,128]{1,0:T(8,128)(2,1)S(1)}, bf16[4096,128]{1,0:T(8,128)(2,1)}, u32[]{:S(2)}) copy-start(bf16[4096,128]{1,0:T(8,128)(2,1)} %param.23) | copy-start | bytes 3145732
  7.2 2.6 copy-start.6
  7.2 3.0 copy-start.13
  7.2 3.1 copy-start.15
  7.2 265.4 %all-gather.5.cloned.1.call-start = ((), (), s32[]{:S(2)}) async-start(), calls=%async_computation.3 | async-start | bytes 2228224 | tf_op jit(solution)/shard_map/all_gather | solution.py:15
  9.7 1.3 copy-start.5
  11.2 1.3 copy-start.16
  11.2 40.2 %copy-start.3 = (s32[8,5632]{1,0:T(8,128)S(1)}, s32[8,5632]{1,0:T(8,128)}, u32[]{:S(2)}) copy-start(s32[8,5632]{1,0:T(8,128)} %param.27) | copy-start | bytes 540676
  11.6 72.5 %copy-start.1 = (bf16[8,176,3,128]{3,1,2,0:T(8,128)(2,1)S(1)}, bf16[8,176,3,128]{3,1,2,0:T(8,128)(2,1)}, u32[]{:S(2)}) copy-start(bf16[8,176,3,128]{3,1,2,0:T(8,128)(2,1)} %param.26) | copy-start | bytes 3244036
  84.2 6.8 copy-start.4
  84.2 6.8 copy-start.11
  84.2 6.9 copy-start.14
  273.6 30.7 %copy-start.8 = (bf16[8,128]{1,0:T(8,128)(2,1)S(1)}, bf16[8,128]{1,0:T(8,128)(2,1)}, u32[]{:S(2)}) copy-start(bf16[8,128]{1,0:T(8,128)(2,1)} %param.17) | copy-start | bytes 6148
  273.6 30.7 %copy-start.10 = (f32[128]{0:T(128)S(1)}, f32[128]{0:T(128)}, u32[]{:S(2)}) copy-start(f32[128]{0:T(128)} %convert_element_type.67) | copy-start | bytes 1540
  305.4 42.9 %all-to-all-start = ((bf16[32,8,128]{2,1,0:T(8,128)(2,1)}), bf16[32,8,128]{2,1,0:T(8,128)(2,1)S(1)}, u32[]{:S(2)}, u32[]{:S(2)}) async-start(bf16[32,8,128]{2,1,0:T(8,128)(2,1)} %stack.2), calls=%async_computation | async-start | bytes 131072 | tf_op jit(solution)/shard_map/all_to_all | solution.py:164
  348.2 466.0 %all-to-all-start.1 = ((bf16[32,44,3,128]{3,1,2,0:T(8,128)(2,1)}), bf16[32,44,3,128]{3,1,2,0:T(8,128)(2,1)}, u32[]{:S(2)}, u32[]{:S(2)}) async-start(bf16[32,44,3,128]{3,1,2,0:T(8,128)(2,1)} %copy.179), calls=%async_computation.1 | async-start | bytes 2359296 | tf_op jit(solution)/shard_map/all_to_all | solution.py:120
  356.0 449.7 %all-reduce.6.cloned.1.call-start = ((), (), s32[]{:S(2)}) async-start(), calls=%async_computation.2 | async-start | bytes 1441792 | tf_op jit(solution)/shard_map/psum | solution.py:189
  521.5 9.7 copy-start.7
  530.1 11.9 %copy-start.12 = (u32[512]{0:T(512)S(1)}, u32[512]{0:T(512)}, u32[]{:S(2)}) copy-start(u32[512]{0:T(512)} %constant.216) | copy-start | bytes 6148
  531.4 96.6 %copy-start.2 = (bf16[8,176,3,128]{3,1,2,0:T(8,128)(2,1)S(1)}, bf16[8,176,3,128]{3,1,2,0:T(8,128)(2,1)}, u32[]{:S(2)}) copy-start(bf16[8,176,3,128]{3,1,2,0:T(8,128)(2,1)} %param.26) | copy-start | bytes 3244036
  642.1 1.4 copy-start.9
  643.4 502.2 %all-reduce.8.cloned.1.call-start = ((), (), s32[]{:S(2)}) async-start(), calls=%async_computation.4 | async-start | bytes 262144
Sparse Core Ops, SparseCore 0:
  12.7 77.0 all-gather.4
  643.5 162.1 all-reduce.5
  813.0 332.5 all-reduce.7
